TPU v7x, 128 devices: a whole 4x4x4 slice. The times are simulated.
128 devices in a mesh: rows: 32 (over y, x, core), cols: 4 (over z).
Axes of the slice: x: 4, y: 4, z: 4, core: 2. Of those that a mesh axis runs over, the one named last changes fastest.
Arguments:
- feats: bfloat16 [131072, 512], P('rows', 'cols'), may hold values from -6 to 6
- adj_vals: bfloat16 [1024, 16, 128, 128], P('rows'), may hold values from -0.125 to 0.125
- colref: int32 [1024, 16], P('rows'), may hold values from 0 to 95, as said below
- fetch_ids: int32 [32, 32, 2], P('rows'), may hold values from -1 to 31, as said below
- w_self: bfloat16 [512, 512], replicated, may hold values from -0.25 to 0.25
- w_neigh: bfloat16 [512, 512], replicated, may hold values from -0.25 to 0.25
- grad_out: bfloat16 [131072, 512], P(('rows', 'cols')), may hold values from -6 to 6
Outputs:
- act_out: bfloat16 [131072, 512], P(('rows', 'cols'))
- grad_self_w: float32 [512, 512], replicated
- grad_neigh_w: float32 [512, 512], replicated
- grad_feats: float32 [131072, 512], P('rows', 'cols')
Inputs may be any that keep to these rules, and one draw needn't show every extreme that they name: `fetch_ids`: entry [r, o, s] is a row tile index within partition o (0 to 31) that partition r reads, or -1 for an empty slot. The entries of one r and o are distinct, all slots with o = r are empty, and every r fills all 2 slots of at least one o. `colref`: entry [b, k], with r = b // 32, is below 32 for partition r's own row tile of that index, or 32 + o * 2 + s for the slot s of fetch_ids[r, o], never an empty slot; so it lies in 0 to 32 + 32 * 2 - 1. The 16 entries of a row tile are distinct and the first is b - r * 32, the row tile itself.
All inputs are finite; a program needn't handle non-finite values.
Results may differ from a plain program's by a relative error of at most 0.0057.
Values may be sent and summed in bfloat16 or wider, within the bound.
A program may use at most 192 MiB of HBM per device.

v0:
```python
import math
import jax
import jax.numpy as jnp
from jax import lax
from jax.sharding import PartitionSpec as P


def body(feats, adj_vals, colref, fetch_ids, w_self, w_neigh, grad_out):
    node_rows, feat_cols = feats.shape
    blocks = adj_vals.shape[0]
    per_block = adj_vals.shape[1]
    tile_rows = adj_vals.shape[2]
    partitions = lax.axis_size("rows")
    capacity = fetch_ids.shape[2]
    total_nodes = node_rows * partitions
    own_tiles = feats.reshape(blocks, tile_rows * feat_cols)
    wanted = lax.all_to_all(fetch_ids, "rows", split_axis=1, concat_axis=0, tiled=True).reshape(
        partitions * capacity
    )
    choose = (wanted[:, None] == jnp.arange(blocks, dtype=jnp.int32)[None, :]).astype(jnp.bfloat16)
    outgoing = jnp.dot(choose, own_tiles, preferred_element_type=jnp.float32).astype(jnp.bfloat16)
    outgoing = outgoing.reshape(partitions, capacity, tile_rows, feat_cols)
    arrived = lax.all_to_all(outgoing, "rows", split_axis=0, concat_axis=0, tiled=True)
    tile_pool = jnp.concatenate(
        [
            feats.reshape(blocks, tile_rows, feat_cols),
            arrived.reshape(partitions * capacity, tile_rows, feat_cols),
        ],
        axis=0,
    )
    picked = jnp.take(tile_pool, colref, axis=0)
    aggregated = jnp.einsum("bkij,bkjf->bif", adj_vals, picked, preferred_element_type=jnp.float32)
    aggregated = aggregated.astype(jnp.bfloat16).reshape(node_rows, feat_cols)
    feat_rows, agg_rows = (
        lax.all_to_all(feats, "cols", split_axis=0, concat_axis=1, tiled=True),
        lax.all_to_all(aggregated, "cols", split_axis=0, concat_axis=1, tiled=True),
    )
    preact = jnp.dot(feat_rows, w_self, preferred_element_type=jnp.float32) + jnp.dot(
        agg_rows, w_neigh, preferred_element_type=jnp.float32
    )
    activation, pull_back = jax.vjp(jax.nn.gelu, preact)
    grad_pre = pull_back(grad_out.astype(jnp.float32))[0].astype(jnp.bfloat16)
    contract = (((0,), (0,)), ((), ()))
    weight_terms = (
        lax.dot_general(feat_rows, grad_pre, contract, preferred_element_type=jnp.float32),
        lax.dot_general(agg_rows, grad_pre, contract, preferred_element_type=jnp.float32),
    )
    self_sum, neigh_sum = lax.psum((weight_terms[0], weight_terms[1]), ("rows", "cols"))
    grad_scale = 1.0 / math.sqrt(total_nodes)
    grad_self_w = self_sum * grad_scale
    grad_neigh_w = neigh_sum * grad_scale
    dims_back = (((1,), (1,)), ((), ()))
    column = lax.axis_index("cols") * feat_cols
    self_slice = lax.dynamic_slice_in_dim(w_self, column, feat_cols, 0)
    neigh_slice = lax.dynamic_slice_in_dim(w_neigh, column, feat_cols, 0)
    rows_in = lax.all_gather(grad_pre, "cols", axis=0, tiled=True)
    self_cols = lax.dot_general(rows_in, self_slice, dims_back, preferred_element_type=jnp.float32)
    neigh_cols = lax.dot_general(
        rows_in, neigh_slice, dims_back, preferred_element_type=jnp.float32
    )
    stacked = jnp.concatenate([self_cols, neigh_cols], axis=1).astype(jnp.bfloat16)
    self_part = stacked[:, :feat_cols]
    grad_agg = stacked[:, feat_cols:]
    grad_blocks = grad_agg.reshape(blocks, tile_rows, feat_cols)
    per_ref = jnp.einsum(
        "bkij,bif->bkjf", adj_vals, grad_blocks, preferred_element_type=jnp.float32
    )
    pool_slots = blocks + partitions * capacity
    pick_table = (
        jnp.arange(pool_slots, dtype=jnp.int32)[:, None] == colref.reshape(1, blocks * per_block)
    ).astype(jnp.float32)
    pooled = jnp.dot(
        pick_table,
        per_ref.reshape(blocks * per_block, tile_rows * feat_cols),
        precision=lax.Precision.HIGHEST,
        preferred_element_type=jnp.float32,
    )
    shares = pooled.astype(jnp.bfloat16).reshape(pool_slots, tile_rows, feat_cols)
    remote_shares = shares[blocks:].reshape(partitions, capacity, tile_rows, feat_cols)
    returned = lax.all_to_all(remote_shares, "rows", split_axis=0, concat_axis=0, tiled=True)
    gathered_back = jnp.dot(
        choose.T,
        returned.reshape(partitions * capacity, tile_rows * feat_cols),
        preferred_element_type=jnp.float32,
    )
    grad_feats = self_part.astype(jnp.float32) + shares[:blocks].astype(jnp.float32).reshape(
        node_rows, feat_cols
    )
    grad_feats = grad_feats + gathered_back.reshape(node_rows, feat_cols)
    return (activation.astype(jnp.bfloat16), grad_self_w, grad_neigh_w, grad_feats)


def solution(mesh):
    in_specs = (
        P("rows", "cols"),
        P("rows", None, None, None),
        P("rows", None),
        P("rows", None, None),
        P(),
        P(),
        P(("rows", "cols"), None),
    )
    out_specs = (P(("rows", "cols"), None), P(), P(), P("rows", "cols"))
    return jax.shard_map(body, mesh=mesh, in_specs=in_specs, out_specs=out_specs, check_vma=False)
```

profile of v0, /device:TPU:0, one launch (start us, length us, event | category | flops | bytes accessed | tf_op | source)
XLA Modules:
  0.0 468.5 jit_solution(2527435484349896378)
XLA Ops:
  9.4 7.4 %all-to-all-start.1 = ((s32[1,32,2]{2,0,1:T(1,128)}), s32[1,32,2]{2,0,1:T(1,128)S(1)}, u32[]{:S(2)}, u32[]{:S(2)}) async-start(s32[1,32,2]{2,0,1:T(1,128)} %copy.40), calls=%async_computation.1 | async-start | bytes 32768 | tf_op jit(solution)/shard_map/all_to_all | solution.py:17
  18.4 5.7 %all-to-all-done.1 = s32[1,32,2]{2,0,1:T(1,128)S(1)} async-done(((s32[1,32,2]{2,0,1:T(1,128)}), s32[1,32,2]{2,0,1:T(1,128)S(1)}, u32[]{:S(2)}, u32[]{:S(2)}) %all-to-all-start.1) | async-done | bytes 288 | tf_op jit(solution)/shard_map/all_to_all | solution.py:17
  26.2 1.9 copy.54
  28.1 4.1 all-to-all-start.2
  32.5 29.7 %all-to-all-done.2 = bf16[32,2,128,128]{3,2,1,0:T(8,128)(2,1)S(1)} async-done(((bf16[32,2,128,128]{3,2,1,0:T(8,128)(2,1)}), bf16[32,2,128,128]{3,2,1,0:T(8,128)(2,1)S(1)}, u32[]{:S(2)}, u32[]{:S(2)}) %all-to-all-start.2) | async-done | bytes 2097184 | tf_op jit(solution)/shard_map/all_to_all | solution.py:23
  62.2 5.3 %all-to-all-start = ((bf16[4,1024,128]{2,1,0:T(8,128)(2,1)}), bf16[4,1024,128]{2,1,0:T(8,128)(2,1)}, u32[]{:S(2)}, u32[]{:S(2)}) async-start(bf16[4,1024,128]{2,1,0:T(8,128)(2,1)} %bitcast), calls=%async_computation | async-start | bytes 2097152 | tf_op jit(solution)/shard_map/all_to_all | solution.py:35
  67.5 3.2 pad_maximum_fusion
  70.7 15.8 %gather_fusion = bf16[512,128,128]{2,1,0:T(8,128)(2,1)} fusion(bf16[96,128,128]{2,1,0:T(8,128)(2,1)} %pad_maximum_fusion, s32[1024]{0:T(1024)S(1)} %pad_clamp_fusion), kind=kCustom, calls=%fused_computation | custom fusion | bytes 33556480 | tf_op jit(solution)/shard_map/jit(_take)/gather | solution.py:31
  86.5 13.0 %bitcast_convert_fusion = bf16[32,128,128]{1,2,0:T(8,128)(2,1)S(1)} fusion(bf16[32,16,128,128]{3,2,1,0:T(8,128)(2,1)} %param.8, bf16[32,16,128,128]{3,2,1,0:T(8,128)(2,1)} %bitcast.60, pred[32,16]{1,0:T(8,128)(4,1)S(1)} %copy.39), kind=kOutput, calls=%fused_computation.35 | convolution fusion | flops 2156396544 | bytes 34603520 | tf_op jit(solution)/shard_map/bkij,bkjf->bif/dot_general | solution.py:32
  100.8 4.9 %all-to-all-start.3 = ((bf16[4,1024,128]{1,2,0:T(8,128)(2,1)}), bf16[4,1024,128]{1,2,0:T(8,128)(2,1)S(1)}, u32[]{:S(2)}, u32[]{:S(2)}) async-start(bf16[4,1024,128]{1,2,0:T(8,128)(2,1)} %copy.42), calls=%async_computation.3 | async-start | bytes 2097152 | tf_op jit(solution)/shard_map/all_to_all | solution.py:36
  107.3 2.1 fusion.37
  109.3 9.3 %all-to-all-done.3 = bf16[4,1024,128]{1,2,0:T(8,128)(2,1)S(1)} async-done(((bf16[4,1024,128]{1,2,0:T(8,128)(2,1)}), bf16[4,1024,128]{1,2,0:T(8,128)(2,1)S(1)}, u32[]{:S(2)}, u32[]{:S(2)}) %all-to-all-start.3) | async-done | bytes 1048608 | tf_op jit(solution)/shard_map/all_to_all | solution.py:36
  119.6 5.4 %fusion.15 = (bf16[1024,512]{1,0:T(8,128)(2,1)S(1)}, bf16[1024,512]{1,0:T(8,128)(2,1)}) fusion(bf16[1024,512]{1,0:T(8,128)(2,1)} %param.13, f32[1024,512]{1,0:T(8,128)} %fusion.37, bf16[1024,512]{0,1:T(8,128)(2,1)} %bitcast.66, bf16[512,512]{1,0:T(8,128)(2,1)S(1)} %copy-done), kind=kOutput, calls=%fused_computation.23 | convolution fusion | flops 549453824 | bytes 6815744 | tf_op jit(solution)/shard_map/dot_general | solution.py:38
  129.2 174.5 %all-reduce.3.cloned.1.call-done = (f32[512,512]{0,1:T(8,128)}, f32[512,512]{0,1:T(8,128)}) async-done(((f32[512,512]{0,1:T(8,128)}, f32[512,512]{0,1:T(8,128)}), (f32[512,512]{0,1:T(8,128)}, f32[512,512]{0,1:T(8,128)})) %all-reduce.3.cloned.1.call-update) | async-done | bytes 2097168 | tf_op jit(solution)/shard_map/psum | solution.py:48
  308.1 3.4 convolution_convert_fusion.1
  311.6 21.4 %convolution_bitcast_fusion = f32[32,16,128,128]{2,3,1,0:T(8,128)} fusion(bf16[32,128,128,1]{2,1,3,0:T(8,128)(2,1)S(1)} %bitcast.63, bf16[32,16,128,128]{3,2,1,0:T(8,128)(2,1)} %param.8), kind=kOutput, calls=%fused_computation.9 | convolution fusion | flops 2147483648 | bytes 51380224 | tf_op jit(solution)/shard_map/bkij,bif->bkjf/dot_general | solution.py:65
  333.0 33.4 %copy.46 = f32[32,16,128,128]{3,2,1,0:T(8,128)} copy(f32[32,16,128,128]{2,3,1,0:T(8,128)} %convolution_bitcast_fusion) | data formatting | bytes 67108864 | tf_op jit(solution)/shard_map/bkij,bif->bkjf/dot_general | solution.py:65
  366.4 42.4 %fusion.3 = bf16[96,16384]{1,0:T(8,128)(2,1)} fusion(f32[64,8,128,128]{3,2,1,0:T(8,128)} %bitcast.59, s32[512]{0:T(512)S(1)} %eq.35), kind=kOutput, calls=%fused_computation.4 | convolution fusion | flops 9665298432 | bytes 36702208 | tf_op jit(solution)/shard_map/dot_general | solution.py:72
  412.4 6.0 %all-to-all-start.4 = ((bf16[32,2,128,128]{3,2,1,0:T(8,128)(2,1)}), bf16[32,2,128,128]{3,2,1,0:T(8,128)(2,1)}, u32[]{:S(2)}, u32[]{:S(2)}) async-start(bf16[32,2,128,128]{3,2,1,0:T(8,128)(2,1)} %bitcast.29), calls=%async_computation.4 | async-start | bytes 4194304 | tf_op jit(solution)/shard_map/all_to_all | solution.py:80
  418.4 2.7 slice_convert_fusion
  422.8 25.6 %all-to-all-done.4 = bf16[32,2,128,128]{3,2,1,0:T(8,128)(2,1)} async-done(((bf16[32,2,128,128]{3,2,1,0:T(8,128)(2,1)}), bf16[32,2,128,128]{3,2,1,0:T(8,128)(2,1)}, u32[]{:S(2)}, u32[]{:S(2)}) %all-to-all-start.4) | async-done | bytes 2097184 | tf_op jit(solution)/shard_map/all_to_all | solution.py:80
  448.4 4.4 fusion.23
  452.8 2.7 reshape.71
  455.5 5.5 %fusion.12 = f32[4096,128]{1,0:T(8,128)} fusion(f32[4096,128]{1,0:T(8,128)} %reshape.71, f32[4096,128]{1,0:T(8,128)S(1)} %reshape.72, bf16[4096,512]{1,0:T(8,128)(2,1)} %all-gather.2.cloned.1.call-done, bf16[512,512]{1,0:T(8,128)(2,1)S(1)} %copy-done.5, s32[]{:T(128)S(6)} %select_n.15), kind=kOutput, calls=%fused_computation.15 | convolution fusion | flops 538968064 | bytes 10616836 | tf_op jit(solution)/shard_map/dot_general | solution.py:57
  (44 shorter events, 23.0 us)
Async XLA Ops:
  8.0 111.6 %copy-start = (bf16[512,512]{1,0:T(8,128)(2,1)S(1)}, bf16[512,512]{1,0:T(8,128)(2,1)}, u32[]{:S(2)}) copy-start(bf16[512,512]{1,0:T(8,128)(2,1)} %param.12) | copy-start | bytes 1572868
  9.4 14.7 %all-to-all-start.1 = ((s32[1,32,2]{2,0,1:T(1,128)}), s32[1,32,2]{2,0,1:T(1,128)S(1)}, u32[]{:S(2)}, u32[]{:S(2)}) async-start(s32[1,32,2]{2,0,1:T(1,128)} %copy.40), calls=%async_computation.1 | async-start | bytes 32768 | tf_op jit(solution)/shard_map/all_to_all | solution.py:17
  28.1 4.2 copy-start.6
  28.1 34.1 %all-to-all-start.2 = ((bf16[32,2,128,128]{3,2,1,0:T(8,128)(2,1)}), bf16[32,2,128,128]{3,2,1,0:T(8,128)(2,1)S(1)}, u32[]{:S(2)}, u32[]{:S(2)}) async-start(bf16[32,2,128,128]{3,2,1,0:T(8,128)(2,1)} %bitcast.62), calls=%async_computation.2 | async-start | bytes 4194304 | tf_op jit(solution)/shard_map/all_to_all | solution.py:23
  62.2 38.6 %all-to-all-start = ((bf16[4,1024,128]{2,1,0:T(8,128)(2,1)}), bf16[4,1024,128]{2,1,0:T(8,128)(2,1)}, u32[]{:S(2)}, u32[]{:S(2)}) async-start(bf16[4,1024,128]{2,1,0:T(8,128)(2,1)} %bitcast), calls=%async_computation | async-start | bytes 2097152 | tf_op jit(solution)/shard_map/all_to_all | solution.py:35
  100.8 6.4 %copy-start.5 = (bf16[512,512]{1,0:T(8,128)(2,1)S(1)}, bf16[512,512]{1,0:T(8,128)(2,1)}, u32[]{:S(2)}) copy-start(bf16[512,512]{1,0:T(8,128)(2,1)} %param.11) | copy-start | bytes 1572868
  100.8 17.8 %all-to-all-start.3 = ((bf16[4,1024,128]{1,2,0:T(8,128)(2,1)}), bf16[4,1024,128]{1,2,0:T(8,128)(2,1)S(1)}, u32[]{:S(2)}, u32[]{:S(2)}) async-start(bf16[4,1024,128]{1,2,0:T(8,128)(2,1)} %copy.42), calls=%async_computation.3 | async-start | bytes 2097152 | tf_op jit(solution)/shard_map/all_to_all | solution.py:36
  105.8 198.0 %all-reduce.3.cloned.1.call-start = ((), (), s32[]{:S(2)}) async-start(), calls=%async_computation.6 | async-start | bytes 4194304 | tf_op jit(solution)/shard_map/psum | solution.py:48
  118.6 1.0 copy-start.3
  125.0 3.5 copy-start.2
  125.0 1.7 copy-start.4
  128.5 179.7 %all-gather.2.cloned.1.call-start = ((), (), s32[]{:S(2)}) async-start(), calls=%async_computation.5 | async-start | bytes 5242880 | tf_op jit(solution)/shard_map/all_gather | solution.py:56
  412.4 35.9 %all-to-all-start.4 = ((bf16[32,2,128,128]{3,2,1,0:T(8,128)(2,1)}), bf16[32,2,128,128]{3,2,1,0:T(8,128)(2,1)}, u32[]{:S(2)}, u32[]{:S(2)}) async-start(bf16[32,2,128,128]{3,2,1,0:T(8,128)(2,1)} %bitcast.29), calls=%async_computation.4 | async-start | bytes 4194304 | tf_op jit(solution)/shard_map/all_to_all | solution.py:80
  455.5 5.5 %copy-start.1 = (bf16[512,512]{1,0:T(8,128)(2,1)S(1)}, bf16[512,512]{1,0:T(8,128)(2,1)}, u32[]{:S(2)}) copy-start(bf16[512,512]{1,0:T(8,128)(2,1)} %param.12) | copy-start | bytes 1572868
Sparse Core Ops, SparseCore 0:
  128.6 175.0 all-reduce.2
Sparse Core Ops, SparseCore 1:
  131.2 46.4 all-gather.1
where the time goes:
time: 470 us; the launch traced here: 468 us
  waiting for transfers between devices  245 us (52%)
  matrix products  102 us (22%)
  local copies, waits for them, and re-layouts  69.5 us (15%)
  starting transfers between devices  27.8 us (6%)
  between operations  15.6 us (3%)
  other arithmetic  8.32 us (2%)
    psum x1, waiting for transfers between devices, body(): lax.psum((weight_terms[0], weight_terms[1]), ('rows', 'cols'))  175 us
    dot_general x1, matrix products, body(): jnp.dot(pick_table, per_ref.reshape(blocks * per_block, tile_rows * feat_...  42.4 us
    dot_general x1, local copies, waits for them, and re-layouts, body(): jnp.einsum('bkij,bif->bkjf', adj_vals, grad_blocks, preferred_element_typ...  33.4 us
    all_to_all x1, waiting for transfers between devices, body(): lax.all_to_all(outgoing, 'rows', split_axis=0, concat_axis=0, tiled=True)  29.7 us
    all_to_all x1, waiting for transfers between devices, body(): lax.all_to_all(remote_shares, 'rows', split_axis=0, concat_axis=0, tiled=...  25.6 us
    dot_general x1, matrix products, body(): jnp.einsum('bkij,bif->bkjf', adj_vals, grad_blocks, preferred_element_typ...  21.4 us
    gather x1, local copies, waits for them, and re-layouts, body(): picked = jnp.take(tile_pool, colref, axis=0)  15.8 us
    dot_general x1, matrix products, body(): jnp.einsum('bkij,bkjf->bif', adj_vals, picked, preferred_element_type=jnp...  13 us
  transfers between devices with their start and end apart: 7, of which 5 were waited for; matrix products, arithmetic and copies ran while one was open for 10% of the time, Pallas kernels for 0%

commit v1 on v0

--- a/solution.py
+++ b/solution.py
@@ -45,7 +45,8 @@
         lax.dot_general(feat_rows, grad_pre, contract, preferred_element_type=jnp.float32),
         lax.dot_general(agg_rows, grad_pre, contract, preferred_element_type=jnp.float32),
     )
-    self_sum, neigh_sum = lax.psum((weight_terms[0], weight_terms[1]), ("rows", "cols"))
+    _map_rows = lambda x_local: lax.psum(lax.psum(x_local, "rows"), "cols")
+    self_sum, neigh_sum = _map_rows((weight_terms[0], weight_terms[1]))
     grad_scale = 1.0 / math.sqrt(total_nodes)
     grad_self_w = self_sum * grad_scale
     grad_neigh_w = neigh_sum * grad_scale

time: 470 us -> 506 us (1.077)
  waiting for transfers between devices: 245 us -> 282 us
    all_gather x1, waiting for transfers between devices: 0.01 us -> 46.1 us  [body(): rows_in = lax.all_gather(grad_pre, 'cols', axis=0, tiled=True)]
    psum x1 -> x2, waiting for transfers between devices: 175 us -> 165 us  [body(): _map_rows = lambda x_local: lax.psum(lax.psum(x_local, 'rows'), 'cols')]
  transfers between devices with their start and end apart: 7 -> 8, of which waited for: 5 -> 7; matrix products, arithmetic and copies ran while one was open for 10% -> 9% of each run, Pallas kernels for 0% -> 0%
where the time goes in v1:
time: 506 us; the launch traced here: 505 us
  waiting for transfers between devices  282 us (56%)
  matrix products  102 us (20%)
  local copies, waits for them, and re-layouts  69.5 us (14%)
  starting transfers between devices  29.1 us (6%)
  between operations  13.9 us (3%)
  other arithmetic  8.32 us (2%)
    psum x2, waiting for transfers between devices, body(): _map_rows = lambda x_local: lax.psum(lax.psum(x_local, 'rows'), 'cols')  165 us
    all_gather x1, waiting for transfers between devices, body(): rows_in = lax.all_gather(grad_pre, 'cols', axis=0, tiled=True)  46.1 us
    dot_general x1, matrix products, body(): jnp.dot(pick_table, per_ref.reshape(blocks * per_block, tile_rows * feat_...  42.4 us
    dot_general x1, local copies, waits for them, and re-layouts, body(): jnp.einsum('bkij,bif->bkjf', adj_vals, grad_blocks, preferred_element_typ...  33.4 us
    all_to_all x1, waiting for transfers between devices, body(): lax.all_to_all(outgoing, 'rows', split_axis=0, concat_axis=0, tiled=True)  29.7 us
    all_to_all x1, waiting for transfers between devices, body(): lax.all_to_all(remote_shares, 'rows', split_axis=0, concat_axis=0, tiled=...  25.6 us
    dot_general x1, matrix products, body(): jnp.einsum('bkij,bif->bkjf', adj_vals, grad_blocks, preferred_element_typ...  21.4 us
    gather x1, local copies, waits for them, and re-layouts, body(): picked = jnp.take(tile_pool, colref, axis=0)  15.8 us
  transfers between devices with their start and end apart: 8, of which 7 were waited for; matrix products, arithmetic and copies ran while one was open for 9% of the time, Pallas kernels for 0%

profile of v1, /device:TPU:0, one launch (start us, length us, event | category | flops | bytes accessed | tf_op | source)
XLA Modules:
  0.0 505.0 jit_solution(9500874507125019641)
XLA Ops:
  8.6 7.4 %all-to-all-start.1 = ((s32[1,32,2]{2,0,1:T(1,128)}), s32[1,32,2]{2,0,1:T(1,128)S(1)}, u32[]{:S(2)}, u32[]{:S(2)}) async-start(s32[1,32,2]{2,0,1:T(1,128)} %copy.40), calls=%async_computation.1 | async-start | bytes 32768 | tf_op jit(solution)/shard_map/all_to_all | solution.py:17
  17.5 5.7 %all-to-all-done.1 = s32[1,32,2]{2,0,1:T(1,128)S(1)} async-done(((s32[1,32,2]{2,0,1:T(1,128)}), s32[1,32,2]{2,0,1:T(1,128)S(1)}, u32[]{:S(2)}, u32[]{:S(2)}) %all-to-all-start.1) | async-done | bytes 288 | tf_op jit(solution)/shard_map/all_to_all | solution.py:17
  27.3 4.1 all-to-all-start.2
  31.7 29.7 %all-to-all-done.2 = bf16[32,2,128,128]{3,2,1,0:T(8,128)(2,1)S(1)} async-done(((bf16[32,2,128,128]{3,2,1,0:T(8,128)(2,1)}), bf16[32,2,128,128]{3,2,1,0:T(8,128)(2,1)S(1)}, u32[]{:S(2)}, u32[]{:S(2)}) %all-to-all-start.2) | async-done | bytes 2097184 | tf_op jit(solution)/shard_map/all_to_all | solution.py:23
  61.4 5.3 %all-to-all-start = ((bf16[4,1024,128]{2,1,0:T(8,128)(2,1)}), bf16[4,1024,128]{2,1,0:T(8,128)(2,1)}, u32[]{:S(2)}, u32[]{:S(2)}) async-start(bf16[4,1024,128]{2,1,0:T(8,128)(2,1)} %bitcast), calls=%async_computation | async-start | bytes 2097152 | tf_op jit(solution)/shard_map/all_to_all | solution.py:35
  66.7 3.2 pad_maximum_fusion
  69.9 15.8 %gather_fusion = bf16[512,128,128]{2,1,0:T(8,128)(2,1)} fusion(bf16[96,128,128]{2,1,0:T(8,128)(2,1)} %pad_maximum_fusion, s32[1024]{0:T(1024)S(1)} %pad_clamp_fusion), kind=kCustom, calls=%fused_computation | custom fusion | bytes 33556480 | tf_op jit(solution)/shard_map/jit(_take)/gather | solution.py:31
  85.7 13.0 %bitcast_convert_fusion = bf16[32,128,128]{1,2,0:T(8,128)(2,1)S(1)} fusion(bf16[32,16,128,128]{3,2,1,0:T(8,128)(2,1)} %param.8, bf16[32,16,128,128]{3,2,1,0:T(8,128)(2,1)} %bitcast.60, pred[32,16]{1,0:T(8,128)(4,1)S(1)} %copy.39), kind=kOutput, calls=%fused_computation.35 | convolution fusion | flops 2156396544 | bytes 34603520 | tf_op jit(solution)/shard_map/bkij,bkjf->bif/dot_general | solution.py:32
  100.0 4.9 all-to-all-start.3
  108.5 9.3 %all-to-all-done.3 = bf16[4,1024,128]{1,2,0:T(8,128)(2,1)S(1)} async-done(((bf16[4,1024,128]{1,2,0:T(8,128)(2,1)}), bf16[4,1024,128]{1,2,0:T(8,128)(2,1)S(1)}, u32[]{:S(2)}, u32[]{:S(2)}) %all-to-all-start.3) | async-done | bytes 1048608 | tf_op jit(solution)/shard_map/all_to_all | solution.py:36
  118.8 5.4 %fusion.15 = (bf16[1024,512]{1,0:T(8,128)(2,1)S(1)}, bf16[1024,512]{1,0:T(8,128)(2,1)}) fusion(bf16[1024,512]{1,0:T(8,128)(2,1)} %param.13, f32[1024,512]{1,0:T(8,128)} %fusion.37, bf16[1024,512]{0,1:T(8,128)(2,1)} %bitcast.66, bf16[512,512]{1,0:T(8,128)(2,1)S(1)} %copy-done), kind=kOutput, calls=%fused_computation.23 | convolution fusion | flops 549453824 | bytes 6815744 | tf_op jit(solution)/shard_map/dot_general | solution.py:38
  127.7 104.8 %all-reduce.5.cloned.1.call-done = (f32[512,512]{0,1:T(8,128)}, f32[512,512]{0,1:T(8,128)}) async-done(((f32[512,512]{0,1:T(8,128)}, f32[512,512]{0,1:T(8,128)}), (f32[512,512]{0,1:T(8,128)}, f32[512,512]{0,1:T(8,128)})) %all-reduce.5.cloned.1.call-update) | async-done | bytes 2097168 | tf_op jit(solution)/shard_map/psum | solution.py:48
  233.4 60.4 %all-reduce.7.cloned.1.call-done = (f32[512,512]{0,1:T(8,128)}, f32[512,512]{0,1:T(8,128)}) async-done(((f32[512,512]{0,1:T(8,128)}, f32[512,512]{0,1:T(8,128)}), (f32[512,512]{0,1:T(8,128)}, f32[512,512]{0,1:T(8,128)})) %all-reduce.7.cloned.1.call-update) | async-done | bytes 2097168 | tf_op jit(solution)/shard_map/psum | solution.py:48
  298.2 46.1 %all-gather.2.cloned.1.call-done = bf16[4096,512]{1,0:T(8,128)(2,1)} async-done(((bf16[1024,512]{1,0:T(8,128)(2,1)}), bf16[4096,512]{1,0:T(8,128)(2,1)}) %all-gather.2.cloned.1.call-update) | async-done | bytes 4194320 | tf_op jit(solution)/shard_map/all_gather | solution.py:57
  344.3 3.4 convolution_convert_fusion.1
  347.8 21.4 %convolution_bitcast_fusion = f32[32,16,128,128]{2,3,1,0:T(8,128)} fusion(bf16[32,128,128,1]{2,1,3,0:T(8,128)(2,1)S(1)} %bitcast.63, bf16[32,16,128,128]{3,2,1,0:T(8,128)(2,1)} %param.8), kind=kOutput, calls=%fused_computation.9 | convolution fusion | flops 2147483648 | bytes 51380224 | tf_op jit(solution)/shard_map/bkij,bif->bkjf/dot_general | solution.py:66
  369.1 33.4 %copy.46 = f32[32,16,128,128]{3,2,1,0:T(8,128)} copy(f32[32,16,128,128]{2,3,1,0:T(8,128)} %convolution_bitcast_fusion) | data formatting | bytes 67108864 | tf_op jit(solution)/shard_map/bkij,bif->bkjf/dot_general | solution.py:66
  402.6 42.4 %fusion.3 = bf16[96,16384]{1,0:T(8,128)(2,1)} fusion(f32[64,8,128,128]{3,2,1,0:T(8,128)} %bitcast.59, s32[512]{0:T(512)S(1)} %eq.35), kind=kOutput, calls=%fused_computation.4 | convolution fusion | flops 9665298432 | bytes 36702208 | tf_op jit(solution)/shard_map/dot_general | solution.py:73
  448.7 7.2 %all-to-all-start.4 = ((bf16[32,2,128,128]{3,2,1,0:T(8,128)(2,1)}), bf16[32,2,128,128]{3,2,1,0:T(8,128)(2,1)}, u32[]{:S(2)}, u32[]{:S(2)}) async-start(bf16[32,2,128,128]{3,2,1,0:T(8,128)(2,1)} %bitcast.29), calls=%async_computation.4 | async-start | bytes 4194304 | tf_op jit(solution)/shard_map/all_to_all | solution.py:81
  455.9 2.7 slice_convert_fusion
  460.3 25.6 %all-to-all-done.4 = bf16[32,2,128,128]{3,2,1,0:T(8,128)(2,1)} async-done(((bf16[32,2,128,128]{3,2,1,0:T(8,128)(2,1)}), bf16[32,2,128,128]{3,2,1,0:T(8,128)(2,1)}, u32[]{:S(2)}, u32[]{:S(2)}) %all-to-all-start.4) | async-done | bytes 2097184 | tf_op jit(solution)/shard_map/all_to_all | solution.py:81
  485.9 4.4 fusion.23
  490.3 2.7 reshape.71
  493.0 5.5 %fusion.12 = f32[4096,128]{1,0:T(8,128)} fusion(f32[4096,128]{1,0:T(8,128)} %reshape.71, f32[4096,128]{1,0:T(8,128)S(1)} %reshape.72, bf16[4096,512]{1,0:T(8,128)(2,1)} %all-gather.2.cloned.1.call-done, bf16[512,512]{1,0:T(8,128)(2,1)S(1)} %copy-done.5, s32[]{:T(128)S(6)} %select_n.15), kind=kOutput, calls=%fused_computation.15 | convolution fusion | flops 538968064 | bytes 10616836 | tf_op jit(solution)/shard_map/dot_general | solution.py:58
  (47 shorter events, 27.2 us)
Async XLA Ops:
  7.2 111.6 %copy-start = (bf16[512,512]{1,0:T(8,128)(2,1)S(1)}, bf16[512,512]{1,0:T(8,128)(2,1)}, u32[]{:S(2)}) copy-start(bf16[512,512]{1,0:T(8,128)(2,1)} %param.12) | copy-start | bytes 1572868
  8.6 14.7 %all-to-all-start.1 = ((s32[1,32,2]{2,0,1:T(1,128)}), s32[1,32,2]{2,0,1:T(1,128)S(1)}, u32[]{:S(2)}, u32[]{:S(2)}) async-start(s32[1,32,2]{2,0,1:T(1,128)} %copy.40), calls=%async_computation.1 | async-start | bytes 32768 | tf_op jit(solution)/shard_map/all_to_all | solution.py:17
  27.3 4.2 copy-start.6
  27.3 34.1 %all-to-all-start.2 = ((bf16[32,2,128,128]{3,2,1,0:T(8,128)(2,1)}), bf16[32,2,128,128]{3,2,1,0:T(8,128)(2,1)S(1)}, u32[]{:S(2)}, u32[]{:S(2)}) async-start(bf16[32,2,128,128]{3,2,1,0:T(8,128)(2,1)} %bitcast.62), calls=%async_computation.2 | async-start | bytes 4194304 | tf_op jit(solution)/shard_map/all_to_all | solution.py:23
  61.4 38.6 %all-to-all-start = ((bf16[4,1024,128]{2,1,0:T(8,128)(2,1)}), bf16[4,1024,128]{2,1,0:T(8,128)(2,1)}, u32[]{:S(2)}, u32[]{:S(2)}) async-start(bf16[4,1024,128]{2,1,0:T(8,128)(2,1)} %bitcast), calls=%async_computation | async-start | bytes 2097152 | tf_op jit(solution)/shard_map/all_to_all | solution.py:35
  100.0 6.4 %copy-start.5 = (bf16[512,512]{1,0:T(8,128)(2,1)S(1)}, bf16[512,512]{1,0:T(8,128)(2,1)}, u32[]{:S(2)}) copy-start(bf16[512,512]{1,0:T(8,128)(2,1)} %param.11) | copy-start | bytes 1572868
  100.0 17.8 %all-to-all-start.3 = ((bf16[4,1024,128]{1,2,0:T(8,128)(2,1)}), bf16[4,1024,128]{1,2,0:T(8,128)(2,1)S(1)}, u32[]{:S(2)}, u32[]{:S(2)}) async-start(bf16[4,1024,128]{1,2,0:T(8,128)(2,1)} %copy.42), calls=%async_computation.3 | async-start | bytes 2097152 | tf_op jit(solution)/shard_map/all_to_all | solution.py:36
  104.9 127.6 %all-reduce.5.cloned.1.call-start = ((), (), s32[]{:S(2)}) async-start(), calls=%async_computation.6 | async-start | bytes 4194304 | tf_op jit(solution)/shard_map/psum | solution.py:48
  117.8 1.0 copy-start.3
  124.1 3.5 copy-start.2
  124.2 1.7 copy-start.4
  127.6 166.2 %all-reduce.7.cloned.1.call-start = ((), (), s32[]{:S(2)}) async-start(), calls=%async_computation.7 | async-start | bytes 4194304 | tf_op jit(solution)/shard_map/psum | solution.py:48
  232.5 111.8 %all-gather.2.cloned.1.call-start = ((), (), s32[]{:S(2)}) async-start(), calls=%async_computation.5 | async-start | bytes 5242880 | tf_op jit(solution)/shard_map/all_gather | solution.py:57
  448.7 37.2 %all-to-all-start.4 = ((bf16[32,2,128,128]{3,2,1,0:T(8,128)(2,1)}), bf16[32,2,128,128]{3,2,1,0:T(8,128)(2,1)}, u32[]{:S(2)}, u32[]{:S(2)}) async-start(bf16[32,2,128,128]{3,2,1,0:T(8,128)(2,1)} %bitcast.29), calls=%async_computation.4 | async-start | bytes 4194304 | tf_op jit(solution)/shard_map/all_to_all | solution.py:81
  493.0 5.5 %copy-start.1 = (bf16[512,512]{1,0:T(8,128)(2,1)S(1)}, bf16[512,512]{1,0:T(8,128)(2,1)}, u32[]{:S(2)}) copy-start(bf16[512,512]{1,0:T(8,128)(2,1)} %param.12) | copy-start | bytes 1572868
Sparse Core Ops, SparseCore 0:
  127.8 104.6 all-reduce.4
  234.9 58.8 all-reduce.6
  296.2 48.1 all-gather.1
